TPU v7x, 256 devices: a whole 4x4x8 slice. The times are simulated.
256 devices in a mesh: fx: 32 (over z, x), fy: 8 (over y, core).
Axes of the slice: x: 4, y: 4, z: 8, core: 2. Of those that a mesh axis runs over, the one named last changes fastest.
Arguments:
- right_side: float32 [4096, 2048], P(('fx', 'fy'))
- coupling: float32 [4096, 11, 4096], P(('fx', 'fy')), may hold values from -0.109375 to 0.109375
- face_columns: int32 [4096, 11], P(('fx', 'fy')), may hold values from 0 to 31, as said below
- ghost_lists: int32 [1024, 4], P(('fx', 'fy')), may hold values from 0 to 15, as said below
Outputs:
- solution: float32 [4096, 2048], P(('fx', 'fy'))
- residual: float32 [4096, 2048], P(('fx', 'fy'))
Inputs may be any that keep to these rules, and one draw needn't show every extreme that they name: face_columns[f, 0] is f's own index within its block; entries 1 to 6 name other faces of the same block, all distinct and below 16; entries 7 to 10 are distinct and name received faces, 16 + d * 4 + g for the g-th face of group d of the extended list; every received slot of every block is named by some row of that block. `ghost_lists`: each row names 4 distinct faces of its block by local index.
All inputs are finite; a program needn't handle non-finite values.
Results may differ from a plain program's by a relative error of at most 0.0003.
Values sent between devices are 32-bit elements; how exact they have to be, the bound alone decides.
No kernel may reach another device: no remote copies, remote signals or barrier semaphores. Data moves between devices by JAX's collectives and lax.ppermute only.
A program may use at most 64 MiB of HBM per device.

v0:
```python
import jax
import jax.numpy as jnp
from jax import lax
from jax.sharding import PartitionSpec as P

DOF = 64
NRHS = 32
BLOCKS = 11
POWERS = 3


def from_behind(block, axis, distance):
    devices = range(lax.axis_size(axis))
    route = [(i - distance, i) for i in devices if i - distance in devices]
    return lax.ppermute(block, axis, route)


def receive_rows(field, ghost_lists):
    from_lower_x = from_behind(jnp.take(field, ghost_lists[1], axis=0), "fx", 1)
    from_upper_x = from_behind(jnp.take(field, ghost_lists[0], axis=0), "fx", -1)
    from_lower_y = from_behind(jnp.take(field, ghost_lists[3], axis=0), "fy", 1)
    from_upper_y = from_behind(jnp.take(field, ghost_lists[2], axis=0), "fy", -1)
    return jnp.concatenate([from_lower_x, from_upper_x, from_lower_y, from_upper_y], axis=0)


def contract(block_mats, picked):
    face_count = picked.shape[0]
    shaped = picked.reshape(face_count, picked.shape[1], DOF, NRHS)
    result = jnp.einsum("fkab,fkbr->far", block_mats, shaped, precision=lax.Precision.HIGHEST)
    return result.reshape(face_count, DOF * NRHS)


def solve_small(gram_total):
    count = NRHS
    row_ids = jnp.arange((POWERS + 1) * count)[:, None]
    col_ids = jnp.arange(POWERS * count)[None, :]
    shift_map = ((row_ids == col_ids) | (row_ids == col_ids + count)).astype(jnp.float32)
    first = (row_ids == jnp.arange(count)[None, :]).astype(jnp.float32)
    high = lax.Precision.HIGHEST
    normal_matrix = jnp.dot(
        shift_map.T, jnp.dot(gram_total, shift_map, precision=high), precision=high
    )
    right_terms = jnp.dot(shift_map.T, gram_total[:, :count], precision=high)
    factor = jnp.linalg.cholesky(normal_matrix)
    coeffs = jax.scipy.linalg.cho_solve((factor, True), right_terms)
    combo = first - jnp.dot(shift_map, coeffs, precision=high)
    return (coeffs, combo)


def on_device(right_side, coupling, face_columns, ghost_lists):
    face_count = right_side.shape[0]
    block_mats = coupling.reshape(face_count, BLOCKS, DOF, DOF)
    high = lax.Precision.HIGHEST

    def as_rows(field):
        return field.reshape(face_count * DOF, NRHS)

    fields = [right_side]
    for power_index in range(POWERS):
        power_field = fields[-1]
        received = receive_rows(power_field, ghost_lists)
        extended = jnp.concatenate([power_field, received], axis=0)
        fields.append(contract(block_mats, jnp.take(extended, face_columns, axis=0)))
    stacked = jnp.concatenate([as_rows(item) for item in fields], axis=1)
    local_gram = jnp.dot(stacked.T, stacked, precision=high, preferred_element_type=jnp.float32)
    gram_total = lax.psum(local_gram, ("fx", "fy"))
    coeffs, combo = solve_small(gram_total)
    solution = jnp.dot(stacked[:, : POWERS * NRHS], coeffs, precision=high)
    residual = jnp.dot(stacked, combo, precision=high)
    return (solution.reshape(face_count, DOF * NRHS), residual.reshape(face_count, DOF * NRHS))


def solution(mesh):
    placed = (
        P(("fx", "fy"), None),
        P(("fx", "fy"), None, None),
        P(("fx", "fy"), None),
        P(("fx", "fy"), None),
    )
    return jax.shard_map(
        on_device,
        mesh=mesh,
        in_specs=placed,
        out_specs=(P(("fx", "fy"), None), P(("fx", "fy"), None)),
        check_vma=False,
    )
```

profile of v0, /device:TPU:1, one launch (start us, length us, event | category | flops | bytes accessed | tf_op | source)
XLA Modules:
  0.0 415.1 jit_solution(4617153673329050650)
XLA Ops:
  7.2 0.8 compare_and_fusion.1
  8.1 1.5 gather_fusion
  9.6 3.9 collective-permute-start
  13.6 1.5 gather_fusion.1
  15.2 1.3 collective-permute-start.1
  16.5 1.5 gather_fusion.2
  18.0 4.0 collective-permute-start.2
  22.1 1.5 gather_fusion.3
  23.7 1.9 collective-permute-start.3
  25.6 0.7 compare_select_fusion
  26.3 0.7 compare_and_fusion
  27.1 5.7 %reshape.61 = f32[16,11,64,64]{3,2,0,1:T(8,128)} reshape(f32[16,11,4096]{2,0,1:T(8,128)} %param.9) | data formatting | bytes 5767168 | tf_op jit(solution)/shard_map/reshape | solution.py:52
  32.9 1.2 gather_fusion.4
  34.1 1.5 reshape.217
  35.6 1.8 broadcast_select_fusion.2
  37.4 3.6 reshape.245
  41.0 12.0 %fusion.6 = f32[16,64,32]{1,2,0:T(8,128)S(1)} fusion(f32[16,11,64,64]{3,2,0,1:T(8,128)} %reshape.61, f32[16,11,64,32]{3,2,1,0:T(8,128)} %reshape.245), kind=kOutput, calls=%fused_computation.21 | convolution fusion | flops 276824064 | bytes 4456448 | tf_op jit(solution)/shard_map/fkab,fkbr->far/dot_general | solution.py:29
  55.8 1.3 collective-permute-start.5
  57.2 3.6 collective-permute-start.6
  60.9 1.9 collective-permute-start.7
  62.9 5.1 %collective-permute-start.4 = (f32[4,2048]{1,0:T(4,128)S(1)}, f32[4,2048]{1,0:T(4,128)S(1)}, u32[]{:S(2)}, u32[]{:S(2)}) collective-permute-start(f32[4,2048]{1,0:T(4,128)S(1)} %broadcast_select_fusion.10), channel_id=1, source_target_pairs={{0,8},{8,16},{16,24},{24,32},{32,40},{40,48},{48,56},{56,64},{64,7... | collective-permute-start | bytes 98312 | tf_op jit(solution)/shard_map/ppermute | solution.py:15
  68.0 0.8 collective-permute-done.4
  68.9 1.2 gather_fusion.9
  70.0 1.6 reshape.229
  71.7 3.2 broadcast_select_fusion.1
  74.9 5.2 %reshape.246 = f32[16,11,64,32]{3,2,1,0:T(8,128)} reshape(f32[16,11,2048]{2,1,0:T(8,128)} %broadcast_select_fusion.1) | data formatting | bytes 2883584 | tf_op jit(solution)/shard_map/reshape | solution.py:28
  80.1 12.0 %fusion.9 = f32[16,64,32]{1,2,0:T(8,128)S(1)} fusion(f32[16,11,64,64]{3,2,0,1:T(8,128)} %reshape.61, f32[16,11,64,32]{3,2,1,0:T(8,128)} %reshape.246), kind=kOutput, calls=%fused_computation.22 | convolution fusion | flops 276824064 | bytes 4456448 | tf_op jit(solution)/shard_map/fkab,fkbr->far/dot_general | solution.py:29
  94.9 4.5 %collective-permute-start.10 = (f32[4,2048]{1,0:T(4,128)S(1)}, f32[4,2048]{1,0:T(4,128)S(1)}, u32[]{:S(2)}, u32[]{:S(2)}) collective-permute-start(f32[4,2048]{1,0:T(4,128)S(1)} %broadcast_select_fusion.4), channel_id=1, source_target_pairs={{0,1},{1,2},{2,3},{3,4},{4,5},{5,6},{6,7},{8,9},{9,10},{10,11},{11... | collective-permute-start | bytes 98312 | tf_op jit(solution)/shard_map/ppermute | solution.py:15
  99.5 1.9 collective-permute-start.11
  101.5 1.3 collective-permute-start.9
  102.9 4.8 %collective-permute-start.8 = (f32[4,2048]{1,0:T(4,128)S(1)}, f32[4,2048]{1,0:T(4,128)S(1)}, u32[]{:S(2)}, u32[]{:S(2)}) collective-permute-start(f32[4,2048]{1,0:T(4,128)S(1)} %broadcast_select_fusion.6), channel_id=1, source_target_pairs={{0,8},{8,16},{16,24},{24,32},{32,40},{40,48},{48,56},{56,64},{64,7... | collective-permute-start | bytes 98312 | tf_op jit(solution)/shard_map/ppermute | solution.py:15
  107.9 0.6 collective-permute-done.8
  108.5 1.2 gather_fusion.14
  109.7 1.6 reshape.241
  111.3 3.2 broadcast_select_fusion
  114.6 5.2 %reshape.247 = f32[16,11,64,32]{3,2,1,0:T(8,128)} reshape(f32[16,11,2048]{2,1,0:T(8,128)} %broadcast_select_fusion) | data formatting | bytes 2883584 | tf_op jit(solution)/shard_map/reshape | solution.py:28
  119.7 12.3 %fusion.12 = f32[16,64,32]{1,2,0:T(8,128)S(1)} fusion(f32[16,11,64,64]{3,2,0,1:T(8,128)} %reshape.61, f32[16,11,64,32]{3,2,1,0:T(8,128)} %reshape.247), kind=kOutput, calls=%fused_computation.23 | convolution fusion | flops 276824064 | bytes 4456448 | tf_op jit(solution)/shard_map/fkab,fkbr->far/dot_general | solution.py:29
  132.7 1.6 fusion.37
  134.4 250.2 %all-reduce.2.cloned.1.call-done = f32[128,128]{1,0:T(8,128)} async-done(((f32[128,128]{1,0:T(8,128)}), f32[128,128]{1,0:T(8,128)}) %all-reduce.2.cloned.1.call-update) | async-done | bytes 65552 | tf_op jit(solution)/shard_map/psum | solution.py:66
  384.6 1.0 fusion.34
  385.9 8.8 %cholesky.16 = f32[96,96]{1,0:T(8,128)S(1)} custom-call(f32[96,96]{1,0:T(8,128)S(1)} %fusion.29), custom_call_target="Cholesky" | custom-call | tf_op jit(solution)/shard_map/jit(cholesky)/cholesky | solution.py:44
  394.8 0.6 compare_reduce_fusion
  395.4 0.7 fusion.24
  396.1 7.4 %custom-call.10 = f32[1,96,96]{1,2,0:T(8,128)S(1)} custom-call(f32[1,96,96]{2,1,0:T(8,128)S(1)} %fusion.24), custom_call_target="InvertDiagBlocksLowerTriangular" | custom-call | tf_op jit(solution)/shard_map/jit(_cho_solve)/triangular_solve | solution.py:45
  403.4 1.1 fusion.21
  405.2 0.7 fusion.15
  406.5 0.9 reshape.67
  407.4 0.9 reshape.66
  (59 shorter events, 9.3 us)
Async XLA Ops:
  7.2 377.4 %all-reduce.2.cloned.1.call-start = ((), (), s32[]{:S(2)}) async-start(), calls=%async_computation | async-start | bytes 131072 | tf_op jit(solution)/shard_map/psum | solution.py:66
  9.6 23.2 %collective-permute-start = (f32[4,2048]{1,0:T(4,128)S(1)}, f32[4,2048]{1,0:T(4,128)S(1)}, u32[]{:S(2)}, u32[]{:S(2)}) collective-permute-start(f32[4,2048]{1,0:T(4,128)S(1)} %broadcast_select_fusion.14), channel_id=1, source_target_pairs={{0,8},{8,16},{16,24},{24,32},{32,40},{40,48},{48,56},{56,64},{64,7... | collective-permute-start | bytes 98312 | tf_op jit(solution)/shard_map/ppermute | solution.py:15
  15.2 17.6 %collective-permute-start.1 = (f32[4,2048]{1,0:T(4,128)S(1)}, f32[4,2048]{1,0:T(4,128)S(1)}, u32[]{:S(2)}, u32[]{:S(2)}) collective-permute-start(f32[4,2048]{1,0:T(4,128)S(1)} %broadcast_select_fusion.13), channel_id=1, source_target_pairs={{8,0},{16,8},{24,16},{32,24},{40,32},{48,40},{56,48},{64,56},{72,6... | collective-permute-start | bytes 98312 | tf_op jit(solution)/shard_map/ppermute | solution.py:15
  18.0 14.8 %collective-permute-start.2 = (f32[4,2048]{1,0:T(4,128)S(1)}, f32[4,2048]{1,0:T(4,128)S(1)}, u32[]{:S(2)}, u32[]{:S(2)}) collective-permute-start(f32[4,2048]{1,0:T(4,128)S(1)} %broadcast_select_fusion.12), channel_id=1, source_target_pairs={{0,1},{1,2},{2,3},{3,4},{4,5},{5,6},{6,7},{8,9},{9,10},{10,11},{11... | collective-permute-start | bytes 98312 | tf_op jit(solution)/shard_map/ppermute | solution.py:15
  23.7 9.2 %collective-permute-start.3 = (f32[4,2048]{1,0:T(4,128)S(1)}, f32[4,2048]{1,0:T(4,128)S(1)}, u32[]{:S(2)}, u32[]{:S(2)}) collective-permute-start(f32[4,2048]{1,0:T(4,128)S(1)} %broadcast_select_fusion.11), channel_id=1, source_target_pairs={{1,0},{2,1},{3,2},{4,3},{5,4},{6,5},{7,6},{9,8},{10,9},{11,10},{12... | collective-permute-start | bytes 98312 | tf_op jit(solution)/shard_map/ppermute | solution.py:15
  27.1 5.7 %copy-start = (f32[16,2048]{1,0:T(8,128)S(1)}, f32[16,2048]{1,0:T(8,128)}, u32[]{:S(2)}) copy-start(f32[16,2048]{1,0:T(8,128)} %param.8) | copy-start | bytes 393220
  55.8 12.2 %collective-permute-start.5 = (f32[4,2048]{1,0:T(4,128)S(1)}, f32[4,2048]{1,0:T(4,128)S(1)}, u32[]{:S(2)}, u32[]{:S(2)}) collective-permute-start(f32[4,2048]{1,0:T(4,128)S(1)} %broadcast_select_fusion.9), channel_id=1, source_target_pairs={{8,0},{16,8},{24,16},{32,24},{40,32},{48,40},{56,48},{64,56},{72,6... | collective-permute-start | bytes 98312 | tf_op jit(solution)/shard_map/ppermute | solution.py:15
  57.2 10.8 %collective-permute-start.6 = (f32[4,2048]{1,0:T(4,128)S(1)}, f32[4,2048]{1,0:T(4,128)S(1)}, u32[]{:S(2)}, u32[]{:S(2)}) collective-permute-start(f32[4,2048]{1,0:T(4,128)S(1)} %broadcast_select_fusion.8), channel_id=1, source_target_pairs={{0,1},{1,2},{2,3},{3,4},{4,5},{5,6},{6,7},{8,9},{9,10},{10,11},{11... | collective-permute-start | bytes 98312 | tf_op jit(solution)/shard_map/ppermute | solution.py:15
  60.9 7.1 %collective-permute-start.7 = (f32[4,2048]{1,0:T(4,128)S(1)}, f32[4,2048]{1,0:T(4,128)S(1)}, u32[]{:S(2)}, u32[]{:S(2)}) collective-permute-start(f32[4,2048]{1,0:T(4,128)S(1)} %broadcast_select_fusion.7), channel_id=1, source_target_pairs={{1,0},{2,1},{3,2},{4,3},{5,4},{6,5},{7,6},{9,8},{10,9},{11,10},{12... | collective-permute-start | bytes 98312 | tf_op jit(solution)/shard_map/ppermute | solution.py:15
  62.9 5.9 %collective-permute-start.4 = (f32[4,2048]{1,0:T(4,128)S(1)}, f32[4,2048]{1,0:T(4,128)S(1)}, u32[]{:S(2)}, u32[]{:S(2)}) collective-permute-start(f32[4,2048]{1,0:T(4,128)S(1)} %broadcast_select_fusion.10), channel_id=1, source_target_pairs={{0,8},{8,16},{16,24},{24,32},{32,40},{40,48},{48,56},{56,64},{64,7... | collective-permute-start | bytes 98312 | tf_op jit(solution)/shard_map/ppermute | solution.py:15
  94.9 12.9 %collective-permute-start.10 = (f32[4,2048]{1,0:T(4,128)S(1)}, f32[4,2048]{1,0:T(4,128)S(1)}, u32[]{:S(2)}, u32[]{:S(2)}) collective-permute-start(f32[4,2048]{1,0:T(4,128)S(1)} %broadcast_select_fusion.4), channel_id=1, source_target_pairs={{0,1},{1,2},{2,3},{3,4},{4,5},{5,6},{6,7},{8,9},{9,10},{10,11},{11... | collective-permute-start | bytes 98312 | tf_op jit(solution)/shard_map/ppermute | solution.py:15
  99.5 8.3 %collective-permute-start.11 = (f32[4,2048]{1,0:T(4,128)S(1)}, f32[4,2048]{1,0:T(4,128)S(1)}, u32[]{:S(2)}, u32[]{:S(2)}) collective-permute-start(f32[4,2048]{1,0:T(4,128)S(1)} %broadcast_select_fusion.3), channel_id=1, source_target_pairs={{1,0},{2,1},{3,2},{4,3},{5,4},{6,5},{7,6},{9,8},{10,9},{11,10},{12... | collective-permute-start | bytes 98312 | tf_op jit(solution)/shard_map/ppermute | solution.py:15
  101.5 6.3 %collective-permute-start.9 = (f32[4,2048]{1,0:T(4,128)S(1)}, f32[4,2048]{1,0:T(4,128)S(1)}, u32[]{:S(2)}, u32[]{:S(2)}) collective-permute-start(f32[4,2048]{1,0:T(4,128)S(1)} %broadcast_select_fusion.5), channel_id=1, source_target_pairs={{8,0},{16,8},{24,16},{32,24},{40,32},{48,40},{56,48},{64,56},{72,6... | collective-permute-start | bytes 98312 | tf_op jit(solution)/shard_map/ppermute | solution.py:15
  102.9 5.6 %collective-permute-start.8 = (f32[4,2048]{1,0:T(4,128)S(1)}, f32[4,2048]{1,0:T(4,128)S(1)}, u32[]{:S(2)}, u32[]{:S(2)}) collective-permute-start(f32[4,2048]{1,0:T(4,128)S(1)} %broadcast_select_fusion.6), channel_id=1, source_target_pairs={{0,8},{8,16},{16,24},{24,32},{32,40},{40,48},{48,56},{56,64},{64,7... | collective-permute-start | bytes 98312 | tf_op jit(solution)/shard_map/ppermute | solution.py:15
Sparse Core Ops, SparseCore 0:
  134.5 250.0 all-reduce.1
where the time goes:
time: 416 us; the launch traced here: 415 us
  waiting for transfers between devices  252 us (61%)
  matrix products  42.2 us (10%)
  local copies, waits for them, and re-layouts  41.9 us (10%)
  starting transfers between devices  35.5 us (9%)
  other arithmetic  29.4 us (7%)
  between operations  14.5 us (3%)
    psum x1, waiting for transfers between devices, on_device(): gram_total = lax.psum(local_gram, ('fx', 'fy'))  250 us
    dot_general x3, matrix products, contract(): jnp.einsum('fkab,fkbr->far', block_mats, shaped, precision=lax.Precision....  36.3 us
    ppermute x12, starting transfers between devices, from_behind(): return lax.ppermute(block, axis, route)  35.5 us
    reshape x3, local copies, waits for them, and re-layouts, contract(): shaped = picked.reshape(face_count, picked.shape[1], DOF, NRHS)  13.9 us
    another operation x3, other arithmetic, solve_small(): factor = jnp.linalg.cholesky(normal_matrix)  9.45 us
    select_n x4, other arithmetic, on_device(): jnp.take(extended, face_columns, axis=0)  8.94 us
  transfers between devices with their start and end apart: 13, of which 3 were waited for; matrix products, arithmetic and copies ran while one was open for 3% of the time, Pallas kernels for 0%

commit v1 on v0

--- a/solution.py
+++ b/solution.py
@@ -63,7 +63,7 @@
         fields.append(contract(block_mats, jnp.take(extended, face_columns, axis=0)))
     stacked = jnp.concatenate([as_rows(item) for item in fields], axis=1)
     local_gram = jnp.dot(stacked.T, stacked, precision=high, preferred_element_type=jnp.float32)
-    gram_total = lax.psum(local_gram, ("fx", "fy"))
+    gram_total = jnp.sum(lax.all_gather(local_gram, ("fx", "fy")), axis=0)
     coeffs, combo = solve_small(gram_total)
     solution = jnp.dot(stacked[:, : POWERS * NRHS], coeffs, precision=high)
     residual = jnp.dot(stacked, combo, precision=high)

time: 416 us -> 308 us (0.74)
  waiting for transfers between devices: 252 us -> 139 us
  other arithmetic: 29.4 us -> 36 us
    psum x1 -> x0, waiting for transfers between devices: 250 us -> none  [on_device(): gram_total = lax.psum(local_gram, ('fx', 'fy'))]
    all_gather x0 -> x1, waiting for transfers between devices: none -> 137 us  [on_device(): gram_total = jnp.sum(lax.all_gather(local_gram, ('fx', 'fy')), axis=0)]
    reduce_sum x0 -> x1, other arithmetic: none -> 6.59 us  [on_device(): gram_total = jnp.sum(lax.all_gather(local_gram, ('fx', 'fy')), axis=0)]
  transfers between devices with their start and end apart: 13 -> 13, of which waited for: 3 -> 3; matrix products, arithmetic and copies ran while one was open for 3% -> 4% of each run, Pallas kernels for 0% -> 0%
where the time goes in v1:
time: 308 us; the launch traced here: 307 us
  waiting for transfers between devices  139 us (45%)
  local copies, waits for them, and re-layouts  41.9 us (14%)
  matrix products  40.5 us (13%)
  other arithmetic  36 us (12%)
  starting transfers between devices  35.5 us (12%)
  between operations  14.5 us (5%)
    all_gather x1, waiting for transfers between devices, on_device(): gram_total = jnp.sum(lax.all_gather(local_gram, ('fx', 'fy')), axis=0)  137 us
    dot_general x3, matrix products, contract(): jnp.einsum('fkab,fkbr->far', block_mats, shaped, precision=lax.Precision....  36.3 us
    ppermute x12, starting transfers between devices, from_behind(): return lax.ppermute(block, axis, route)  35.5 us
    reshape x3, local copies, waits for them, and re-layouts, contract(): shaped = picked.reshape(face_count, picked.shape[1], DOF, NRHS)  13.9 us
    another operation x3, other arithmetic, solve_small(): factor = jnp.linalg.cholesky(normal_matrix)  9.45 us
    select_n x4, other arithmetic, on_device(): jnp.take(extended, face_columns, axis=0)  8.94 us
    gather x6, local copies, waits for them, and re-layouts, on_device(): jnp.take(extended, face_columns, axis=0)  8.28 us
    another operation x2, other arithmetic, solve_small(): coeffs = jax.scipy.linalg.cho_solve((factor, True), right_terms)  8.01 us
  transfers between devices with their start and end apart: 13, of which 3 were waited for; matrix products, arithmetic and copies ran while one was open for 4% of the time, Pallas kernels for 0%

profile of v1, /device:TPU:1, one launch (start us, length us, event | category | flops | bytes accessed | tf_op | source)
XLA Modules:
  0.0 307.3 jit_solution(12428041236761834593)
XLA Ops:
  7.2 0.8 compare_and_fusion.1
  8.1 1.5 gather_fusion
  9.6 3.9 %collective-permute-start = (f32[4,2048]{1,0:T(4,128)S(1)}, f32[4,2048]{1,0:T(4,128)S(1)}, u32[]{:S(2)}, u32[]{:S(2)}) collective-permute-start(f32[4,2048]{1,0:T(4,128)S(1)} %broadcast_select_fusion.14), channel_id=1, source_target_pairs={{0,8},{8,16},{16,24},{24,32},{32,40},{40,48},{48,56},{56,64},{64,7... | collective-permute-start | bytes 98312 | tf_op jit(solution)/shard_map/ppermute | solution.py:15
  13.6 1.5 gather_fusion.1
  15.2 1.3 collective-permute-start.1
  16.5 1.5 gather_fusion.2
  18.0 4.0 %collective-permute-start.2 = (f32[4,2048]{1,0:T(4,128)S(1)}, f32[4,2048]{1,0:T(4,128)S(1)}, u32[]{:S(2)}, u32[]{:S(2)}) collective-permute-start(f32[4,2048]{1,0:T(4,128)S(1)} %broadcast_select_fusion.12), channel_id=1, source_target_pairs={{0,1},{1,2},{2,3},{3,4},{4,5},{5,6},{6,7},{8,9},{9,10},{10,11},{11... | collective-permute-start | bytes 98312 | tf_op jit(solution)/shard_map/ppermute | solution.py:15
  22.1 1.5 gather_fusion.3
  23.7 1.9 collective-permute-start.3
  25.6 0.7 compare_select_fusion
  26.3 0.7 compare_and_fusion
  27.1 5.7 %reshape.61 = f32[16,11,64,64]{3,2,0,1:T(8,128)} reshape(f32[16,11,4096]{2,0,1:T(8,128)} %param.9) | data formatting | bytes 5767168 | tf_op jit(solution)/shard_map/reshape | solution.py:52
  32.9 1.2 gather_fusion.4
  34.1 1.5 reshape.218
  35.6 1.8 broadcast_select_fusion.2
  37.4 3.6 %reshape.246 = f32[16,11,64,32]{3,2,1,0:T(8,128)} reshape(f32[16,11,2048]{2,1,0:T(8,128)S(1)} %broadcast_select_fusion.2) | data formatting | bytes 2883584 | tf_op jit(solution)/shard_map/reshape | solution.py:28
  41.0 12.0 %fusion.6 = f32[16,64,32]{1,2,0:T(8,128)S(1)} fusion(f32[16,11,64,64]{3,2,0,1:T(8,128)} %reshape.61, f32[16,11,64,32]{3,2,1,0:T(8,128)} %reshape.246), kind=kOutput, calls=%fused_computation.21 | convolution fusion | flops 276824064 | bytes 4456448 | tf_op jit(solution)/shard_map/fkab,fkbr->far/dot_general | solution.py:29
  54.6 0.6 gather_fusion.8
  55.8 1.3 collective-permute-start.5
  57.2 3.6 %collective-permute-start.6 = (f32[4,2048]{1,0:T(4,128)S(1)}, f32[4,2048]{1,0:T(4,128)S(1)}, u32[]{:S(2)}, u32[]{:S(2)}) collective-permute-start(f32[4,2048]{1,0:T(4,128)S(1)} %broadcast_select_fusion.8), channel_id=1, source_target_pairs={{0,1},{1,2},{2,3},{3,4},{4,5},{5,6},{6,7},{8,9},{9,10},{10,11},{11... | collective-permute-start | bytes 98312 | tf_op jit(solution)/shard_map/ppermute | solution.py:15
  60.9 1.9 collective-permute-start.7
  62.9 5.1 %collective-permute-start.4 = (f32[4,2048]{1,0:T(4,128)S(1)}, f32[4,2048]{1,0:T(4,128)S(1)}, u32[]{:S(2)}, u32[]{:S(2)}) collective-permute-start(f32[4,2048]{1,0:T(4,128)S(1)} %broadcast_select_fusion.10), channel_id=1, source_target_pairs={{0,8},{8,16},{16,24},{24,32},{32,40},{40,48},{48,56},{56,64},{64,7... | collective-permute-start | bytes 98312 | tf_op jit(solution)/shard_map/ppermute | solution.py:15
  68.0 0.8 collective-permute-done.4
  68.9 1.2 gather_fusion.9
  70.0 1.6 reshape.230
  71.7 3.2 %broadcast_select_fusion.1 = f32[16,11,2048]{2,1,0:T(8,128)} fusion(f32[16,11,2048]{2,1,0:T(8,128)} %reshape.230, pred[16,11]{1,0:T(8,128)(4,1)S(1)} %compare_and_fusion), kind=kLoop, calls=%fused_computation.26 | loop fusion | flops 360448 | bytes 2883760 | tf_op jit(solution)/shard_map/jit(_take)/select_n | solution.py:63
  74.9 5.2 %reshape.247 = f32[16,11,64,32]{3,2,1,0:T(8,128)} reshape(f32[16,11,2048]{2,1,0:T(8,128)} %broadcast_select_fusion.1) | data formatting | bytes 2883584 | tf_op jit(solution)/shard_map/reshape | solution.py:28
  80.1 12.0 %fusion.9 = f32[16,64,32]{1,2,0:T(8,128)S(1)} fusion(f32[16,11,64,64]{3,2,0,1:T(8,128)} %reshape.61, f32[16,11,64,32]{3,2,1,0:T(8,128)} %reshape.247), kind=kOutput, calls=%fused_computation.22 | convolution fusion | flops 276824064 | bytes 4456448 | tf_op jit(solution)/shard_map/fkab,fkbr->far/dot_general | solution.py:29
  94.9 4.5 %collective-permute-start.10 = (f32[4,2048]{1,0:T(4,128)S(1)}, f32[4,2048]{1,0:T(4,128)S(1)}, u32[]{:S(2)}, u32[]{:S(2)}) collective-permute-start(f32[4,2048]{1,0:T(4,128)S(1)} %broadcast_select_fusion.4), channel_id=1, source_target_pairs={{0,1},{1,2},{2,3},{3,4},{4,5},{5,6},{6,7},{8,9},{9,10},{10,11},{11... | collective-permute-start | bytes 98312 | tf_op jit(solution)/shard_map/ppermute | solution.py:15
  99.5 1.9 collective-permute-start.11
  101.5 1.3 collective-permute-start.9
  102.9 4.8 %collective-permute-start.8 = (f32[4,2048]{1,0:T(4,128)S(1)}, f32[4,2048]{1,0:T(4,128)S(1)}, u32[]{:S(2)}, u32[]{:S(2)}) collective-permute-start(f32[4,2048]{1,0:T(4,128)S(1)} %broadcast_select_fusion.6), channel_id=1, source_target_pairs={{0,8},{8,16},{16,24},{24,32},{32,40},{40,48},{48,56},{56,64},{64,7... | collective-permute-start | bytes 98312 | tf_op jit(solution)/shard_map/ppermute | solution.py:15
  107.9 0.6 collective-permute-done.8
  108.5 1.2 gather_fusion.14
  109.7 1.6 reshape.242
  111.3 3.2 %broadcast_select_fusion = f32[16,11,2048]{2,1,0:T(8,128)} fusion(f32[16,11,2048]{2,1,0:T(8,128)} %reshape.242, pred[16,11]{1,0:T(8,128)(4,1)S(1)} %compare_and_fusion), kind=kLoop, calls=%fused_computation.25 | loop fusion | flops 360448 | bytes 2883760 | tf_op jit(solution)/shard_map/jit(_take)/select_n | solution.py:63
  114.6 5.2 %reshape.248 = f32[16,11,64,32]{3,2,1,0:T(8,128)} reshape(f32[16,11,2048]{2,1,0:T(8,128)} %broadcast_select_fusion) | data formatting | bytes 2883584 | tf_op jit(solution)/shard_map/reshape | solution.py:28
  119.7 12.3 %fusion.12 = f32[16,64,32]{1,2,0:T(8,128)S(1)} fusion(f32[16,11,64,64]{3,2,0,1:T(8,128)} %reshape.61, f32[16,11,64,32]{3,2,1,0:T(8,128)} %reshape.248), kind=kOutput, calls=%fused_computation.23 | convolution fusion | flops 276824064 | bytes 4456448 | tf_op jit(solution)/shard_map/fkab,fkbr->far/dot_general | solution.py:29
  132.7 1.6 fusion.37
  134.4 137.5 %all-gather.3.cloned.1.call-done = f32[32768,128]{1,0:T(8,128)} async-done(((f32[128,128]{1,0:T(8,128)}), f32[32768,128]{1,0:T(8,128)}) %all-gather.3.cloned.1.call-update) | async-done | bytes 16777232 | tf_op jit(solution)/shard_map/all_gather | solution.py:66
  271.9 6.6 %reduce_sum.9 = f32[128,128]{1,0:T(8,128)S(1)} reduce(f32[256,128,128]{2,1,0:T(8,128)} %bitcast.54, f32[]{:T(128)} %constant.68.clone.1), dimensions={0}, to_apply=%region_0.3 | reduce | flops 4177920 | bytes 16842756 | tf_op jit(solution)/shard_map/reduce_sum | solution.py:66
  279.2 8.8 %cholesky.16 = f32[96,96]{1,0:T(8,128)S(1)} custom-call(f32[96,96]{1,0:T(8,128)S(1)} %fusion.29), custom_call_target="Cholesky" | custom-call | tf_op jit(solution)/shard_map/jit(cholesky)/cholesky | solution.py:44
  288.0 0.6 compare_reduce_fusion
  288.7 0.7 fusion.24
  289.3 7.4 %custom-call.10 = f32[1,96,96]{1,2,0:T(8,128)S(1)} custom-call(f32[1,96,96]{2,1,0:T(8,128)S(1)} %fusion.24), custom_call_target="InvertDiagBlocksLowerTriangular" | custom-call | tf_op jit(solution)/shard_map/jit(_cho_solve)/triangular_solve | solution.py:45
  297.4 0.7 fusion.15
  298.7 0.9 reshape.67
  299.6 0.9 reshape.66
  (60 shorter events, 9.1 us)
Async XLA Ops:
  7.2 264.7 %all-gather.3.cloned.1.call-start = ((), (), s32[]{:S(2)}) async-start(), calls=%async_computation | async-start | bytes 16842752 | tf_op jit(solution)/shard_map/all_gather | solution.py:66
  9.6 23.2 %collective-permute-start = (f32[4,2048]{1,0:T(4,128)S(1)}, f32[4,2048]{1,0:T(4,128)S(1)}, u32[]{:S(2)}, u32[]{:S(2)}) collective-permute-start(f32[4,2048]{1,0:T(4,128)S(1)} %broadcast_select_fusion.14), channel_id=1, source_target_pairs={{0,8},{8,16},{16,24},{24,32},{32,40},{40,48},{48,56},{56,64},{64,7... | collective-permute-start | bytes 98312 | tf_op jit(solution)/shard_map/ppermute | solution.py:15
  15.2 17.6 %collective-permute-start.1 = (f32[4,2048]{1,0:T(4,128)S(1)}, f32[4,2048]{1,0:T(4,128)S(1)}, u32[]{:S(2)}, u32[]{:S(2)}) collective-permute-start(f32[4,2048]{1,0:T(4,128)S(1)} %broadcast_select_fusion.13), channel_id=1, source_target_pairs={{8,0},{16,8},{24,16},{32,24},{40,32},{48,40},{56,48},{64,56},{72,6... | collective-permute-start | bytes 98312 | tf_op jit(solution)/shard_map/ppermute | solution.py:15
  18.0 14.8 %collective-permute-start.2 = (f32[4,2048]{1,0:T(4,128)S(1)}, f32[4,2048]{1,0:T(4,128)S(1)}, u32[]{:S(2)}, u32[]{:S(2)}) collective-permute-start(f32[4,2048]{1,0:T(4,128)S(1)} %broadcast_select_fusion.12), channel_id=1, source_target_pairs={{0,1},{1,2},{2,3},{3,4},{4,5},{5,6},{6,7},{8,9},{9,10},{10,11},{11... | collective-permute-start | bytes 98312 | tf_op jit(solution)/shard_map/ppermute | solution.py:15
  23.7 9.2 %collective-permute-start.3 = (f32[4,2048]{1,0:T(4,128)S(1)}, f32[4,2048]{1,0:T(4,128)S(1)}, u32[]{:S(2)}, u32[]{:S(2)}) collective-permute-start(f32[4,2048]{1,0:T(4,128)S(1)} %broadcast_select_fusion.11), channel_id=1, source_target_pairs={{1,0},{2,1},{3,2},{4,3},{5,4},{6,5},{7,6},{9,8},{10,9},{11,10},{12... | collective-permute-start | bytes 98312 | tf_op jit(solution)/shard_map/ppermute | solution.py:15
  27.1 5.7 %copy-start = (f32[16,2048]{1,0:T(8,128)S(1)}, f32[16,2048]{1,0:T(8,128)}, u32[]{:S(2)}) copy-start(f32[16,2048]{1,0:T(8,128)} %param.8) | copy-start | bytes 393220
  55.8 12.2 %collective-permute-start.5 = (f32[4,2048]{1,0:T(4,128)S(1)}, f32[4,2048]{1,0:T(4,128)S(1)}, u32[]{:S(2)}, u32[]{:S(2)}) collective-permute-start(f32[4,2048]{1,0:T(4,128)S(1)} %broadcast_select_fusion.9), channel_id=1, source_target_pairs={{8,0},{16,8},{24,16},{32,24},{40,32},{48,40},{56,48},{64,56},{72,6... | collective-permute-start | bytes 98312 | tf_op jit(solution)/shard_map/ppermute | solution.py:15
  57.2 10.8 %collective-permute-start.6 = (f32[4,2048]{1,0:T(4,128)S(1)}, f32[4,2048]{1,0:T(4,128)S(1)}, u32[]{:S(2)}, u32[]{:S(2)}) collective-permute-start(f32[4,2048]{1,0:T(4,128)S(1)} %broadcast_select_fusion.8), channel_id=1, source_target_pairs={{0,1},{1,2},{2,3},{3,4},{4,5},{5,6},{6,7},{8,9},{9,10},{10,11},{11... | collective-permute-start | bytes 98312 | tf_op jit(solution)/shard_map/ppermute | solution.py:15
  60.9 7.1 %collective-permute-start.7 = (f32[4,2048]{1,0:T(4,128)S(1)}, f32[4,2048]{1,0:T(4,128)S(1)}, u32[]{:S(2)}, u32[]{:S(2)}) collective-permute-start(f32[4,2048]{1,0:T(4,128)S(1)} %broadcast_select_fusion.7), channel_id=1, source_target_pairs={{1,0},{2,1},{3,2},{4,3},{5,4},{6,5},{7,6},{9,8},{10,9},{11,10},{12... | collective-permute-start | bytes 98312 | tf_op jit(solution)/shard_map/ppermute | solution.py:15
  62.9 5.9 %collective-permute-start.4 = (f32[4,2048]{1,0:T(4,128)S(1)}, f32[4,2048]{1,0:T(4,128)S(1)}, u32[]{:S(2)}, u32[]{:S(2)}) collective-permute-start(f32[4,2048]{1,0:T(4,128)S(1)} %broadcast_select_fusion.10), channel_id=1, source_target_pairs={{0,8},{8,16},{16,24},{24,32},{32,40},{40,48},{48,56},{56,64},{64,7... | collective-permute-start | bytes 98312 | tf_op jit(solution)/shard_map/ppermute | solution.py:15
  94.9 12.9 %collective-permute-start.10 = (f32[4,2048]{1,0:T(4,128)S(1)}, f32[4,2048]{1,0:T(4,128)S(1)}, u32[]{:S(2)}, u32[]{:S(2)}) collective-permute-start(f32[4,2048]{1,0:T(4,128)S(1)} %broadcast_select_fusion.4), channel_id=1, source_target_pairs={{0,1},{1,2},{2,3},{3,4},{4,5},{5,6},{6,7},{8,9},{9,10},{10,11},{11... | collective-permute-start | bytes 98312 | tf_op jit(solution)/shard_map/ppermute | solution.py:15
  99.5 8.3 %collective-permute-start.11 = (f32[4,2048]{1,0:T(4,128)S(1)}, f32[4,2048]{1,0:T(4,128)S(1)}, u32[]{:S(2)}, u32[]{:S(2)}) collective-permute-start(f32[4,2048]{1,0:T(4,128)S(1)} %broadcast_select_fusion.3), channel_id=1, source_target_pairs={{1,0},{2,1},{3,2},{4,3},{5,4},{6,5},{7,6},{9,8},{10,9},{11,10},{12... | collective-permute-start | bytes 98312 | tf_op jit(solution)/shard_map/ppermute | solution.py:15
  101.5 6.3 %collective-permute-start.9 = (f32[4,2048]{1,0:T(4,128)S(1)}, f32[4,2048]{1,0:T(4,128)S(1)}, u32[]{:S(2)}, u32[]{:S(2)}) collective-permute-start(f32[4,2048]{1,0:T(4,128)S(1)} %broadcast_select_fusion.5), channel_id=1, source_target_pairs={{8,0},{16,8},{24,16},{32,24},{40,32},{48,40},{56,48},{64,56},{72,6... | collective-permute-start | bytes 98312 | tf_op jit(solution)/shard_map/ppermute | solution.py:15
  102.9 5.6 %collective-permute-start.8 = (f32[4,2048]{1,0:T(4,128)S(1)}, f32[4,2048]{1,0:T(4,128)S(1)}, u32[]{:S(2)}, u32[]{:S(2)}) collective-permute-start(f32[4,2048]{1,0:T(4,128)S(1)} %broadcast_select_fusion.6), channel_id=1, source_target_pairs={{0,8},{8,16},{16,24},{24,32},{32,40},{40,48},{48,56},{56,64},{64,7... | collective-permute-start | bytes 98312 | tf_op jit(solution)/shard_map/ppermute | solution.py:15
Sparse Core Ops, SparseCore 0:
  134.5 137.3 all-gather.2
